TPU v7x, 512 devices: a whole 4x4x16 slice. The times are simulated.
512 devices in a mesh: dp: 8 (over x, core), expert: 64 (over z, y).
Axes of the slice: x: 4, y: 4, z: 16, core: 2. Of those that a mesh axis runs over, the one named last changes fastest.
Arguments:
- cells: bfloat16 [131072, 1024], P(('dp', 'expert')), may hold values from -6 to 6
- cell_bins: int32 [131072], P(('dp', 'expert')), may hold values from 0 to 127
- tile_counts: int32 [512, 8], P(('dp', 'expert')), may hold values from 1 to 96, 256 in all within a row
- bin_base: bfloat16 [65536, 1024], P(('dp', 'expert')), may hold values from -6 to 6
- norm_gain: float32 [1024], replicated, may hold values from 0.1 to 1.9
- expert_ids: int32 [65536, 1], P(('dp', 'expert')), may hold values from 0 to 63; in each aligned block of 128 rows (0 to 127, 128 to 255, ...) at most 3 rows name the same one
- gate_q: bfloat16 [64, 4096, 1024], P('expert', 'dp'), may hold values from -0.1875 to 0.1875
- up_q: bfloat16 [64, 4096, 1024], P('expert', 'dp'), may hold values from -0.1875 to 0.1875
- down_q: bfloat16 [64, 4096, 1024], P('expert', 'dp'), may hold values from -0.09375 to 0.09375
- gate_scales: int32 [64, 32, 8], P('expert', 'dp'), may hold values from -1 to 1
- up_scales: int32 [64, 32, 8], P('expert', 'dp'), may hold values from -1 to 1
- down_scales: int32 [64, 32, 8], P('expert', 'dp'), may hold values from -1 to 1
Outputs:
- encoded: bfloat16 [65536, 1024], P(('dp', 'expert'))
Inputs may be any that keep to these rules, and one draw needn't show every extreme that they name: Each device's cells are stored grouped by tile in order of t; row s of tile_counts gives the lengths of these groups, sums to 256, and its largest entry is 96. `expert_ids`: among the 128 bins of one tile no expert is named more than 3 times, a bound that some block reaches.
All inputs are finite; a program needn't handle non-finite values.
Results may differ from a plain program's by a relative error of at most 0.014.
Values may be sent and summed in bfloat16 or wider, within the bound.
No kernel may reach another device: no remote copies, remote signals or barrier semaphores. Data moves between devices by JAX's collectives and lax.ppermute only.
A program may use at most 64 MiB of HBM per device.

v0:
```python
import jax
import jax.numpy as jnp
from jax import lax
from jax.sharding import PartitionSpec as P

QB = 128


def dequantize(quant, scale):
    factor = jnp.exp2(scale.astype(jnp.float32))
    factor = jnp.repeat(jnp.repeat(factor, QB, axis=0), QB, axis=1).astype(jnp.bfloat16)
    return quant * factor


def on_device(
    cells,
    cell_bins,
    tile_counts,
    bin_base,
    norm_gain,
    expert_ids,
    gate_q,
    up_q,
    down_q,
    gate_scales,
    up_scales,
    down_scales,
):
    dp_size = lax.axis_size("dp")
    expert_count = lax.axis_size("expert") * gate_q.shape[0]
    cell_total = cells.shape[0]
    tile_bins = bin_base.shape[0]
    counts = tile_counts[0]
    run_ends = jnp.cumsum(counts)
    run_starts = run_ends - counts
    bin_iota = jnp.arange(tile_bins, dtype=jnp.int32)
    cell_cap = min(3 * cell_total // dp_size, cell_total - dp_size + 1)
    slot_iota = jnp.arange(cell_cap, dtype=jnp.int32)
    take_rows = jnp.clip(run_starts[:, None] + slot_iota[None, :], 0, cell_total - 1).reshape(-1)
    valid = (slot_iota[None, :] < counts[:, None]).reshape(-1)
    slot_rows = jnp.where(
        valid[:, None], jnp.take(cells, take_rows, axis=0), jnp.zeros((), jnp.bfloat16)
    )
    slot_bins = jnp.where(valid, jnp.take(cell_bins, take_rows), -1)
    got_rows, got_bins = (
        lax.all_to_all(slot_rows, "dp", split_axis=0, concat_axis=0, tiled=True),
        lax.all_to_all(slot_bins, "dp", split_axis=0, concat_axis=0, tiled=True),
    )
    matcher = (bin_iota[:, None] == got_bins[None, :]).astype(jnp.bfloat16)
    splat_sum = jnp.dot(matcher, got_rows, preferred_element_type=jnp.float32)
    residual_in = bin_base.astype(jnp.float32) + splat_sum
    mean_sq = jnp.mean(residual_in * residual_in, axis=1, keepdims=True)
    normed = (residual_in * lax.rsqrt(mean_sq + 1e-06) * norm_gain[None, :]).astype(jnp.bfloat16)
    capacity = max(2, 3 * tile_bins // (2 * expert_count))
    expert_col = expert_ids[:, 0]
    one_hot = (expert_col[:, None] == jnp.arange(expert_count, dtype=jnp.int32)[None, :]).astype(
        jnp.int32
    )
    within = jnp.sum(jnp.cumsum(one_hot, axis=0) * one_hot, axis=1) - 1
    slot_of = expert_col * capacity + within
    placer = (
        jnp.arange(expert_count * capacity, dtype=jnp.int32)[:, None] == slot_of[None, :]
    ).astype(jnp.bfloat16)
    outgoing = jnp.dot(placer, normed, preferred_element_type=jnp.float32).astype(jnp.bfloat16)
    arrived = lax.all_to_all(outgoing, "expert", split_axis=0, concat_axis=0, tiled=True)
    w_gate = dequantize(gate_q[0], gate_scales[0])
    w_up = dequantize(up_q[0], up_scales[0])
    w_down = dequantize(down_q[0], down_scales[0])
    contract = (((1,), (1,)), ((), ()))
    block_rows = lax.all_gather(arrived, "dp", axis=0, tiled=True)
    gate_val = lax.dot_general(block_rows, w_gate, contract, preferred_element_type=jnp.float32)
    up_val = lax.dot_general(block_rows, w_up, contract, preferred_element_type=jnp.float32)
    hidden = (jax.nn.silu(gate_val) * up_val).astype(jnp.bfloat16)
    partial_rows = jnp.dot(hidden, w_down, preferred_element_type=jnp.float32)
    summed = lax.psum_scatter(
        partial_rows.astype(jnp.bfloat16), "dp", scatter_dimension=0, tiled=True
    )
    returned = lax.all_to_all(summed, "expert", split_axis=0, concat_axis=0, tiled=True)
    expert_out = lax.dot_general(
        placer, returned, (((0,), (0,)), ((), ())), preferred_element_type=jnp.float32
    )
    return (residual_in + expert_out).astype(jnp.bfloat16)


def solution(mesh):
    placed = (
        P(("dp", "expert"), None),
        P(("dp", "expert")),
        P(("dp", "expert"), None),
        P(("dp", "expert"), None),
        P(),
        P(("dp", "expert"), None),
        P("expert", "dp", None),
        P("expert", "dp", None),
        P("expert", "dp", None),
        P("expert", "dp", None),
        P("expert", "dp", None),
        P("expert", "dp", None),
    )
    return jax.shard_map(
        on_device, mesh=mesh, in_specs=placed, out_specs=P(("dp", "expert"), None), check_vma=False
    )
```

profile of v0, /device:TPU:7, one launch (start us, length us, event | category | flops | bytes accessed | tf_op | source)
XLA Modules:
  0.0 243.5 jit_solution(11036003348992583538)
XLA Ops:
  6.5 0.0 copy-start
  6.5 0.9 reduce-window.8
  7.4 0.7 bitcast_subtract_fusion
  8.1 0.1 add_clamp_fusion
  8.2 0.1 min.18
  8.3 4.8 %gather_fusion = s32[768]{0:T(1024)S(1)} fusion(s32[256]{0:T(256)} %param.13, s32[1024]{0:T(1024)S(1)} %pad_clamp_fusion), kind=kCustom, calls=%fused_computation | custom fusion | bytes 9216 | tf_op jit(solution)/shard_map/jit(_take)/gather | solution.py:44
  13.1 0.1 gather.13
  13.2 0.0 copy-done.7
  13.2 0.7 select_select_fusion.1
  13.9 9.4 %all-to-all-start = ((s32[8,96,1]{1,2,0:T(1,128)}), s32[8,96,1]{1,2,0:T(1,128)S(1)}, u32[]{:S(2)}, u32[]{:S(2)}) async-start(s32[8,96,1]{1,2,0:T(1,128)} %bitcast.3), calls=%async_computation | async-start | bytes 8192 | tf_op jit(solution)/shard_map/all_to_all | solution.py:47
  23.3 0.1 iota_compare_fusion.6
  23.3 0.0 copy-done
  23.3 2.8 %gather_fusion.1 = bf16[768,1024]{1,0:T(8,128)(2,1)S(1)} fusion(bf16[256,1024]{1,0:T(8,128)(2,1)S(1)} %copy-done, s32[1024]{0:T(1024)S(1)} %pad_clamp_fusion), kind=kCustom, calls=%fused_computation.1 | custom fusion | bytes 3148800 | tf_op jit(solution)/shard_map/jit(_take)/gather | solution.py:42
  26.2 0.0 copy-start.3
  26.2 0.0 copy-start.1
  26.2 1.5 select_select_fusion
  27.6 0.0 all-to-all-done
  27.6 4.9 %all-to-all-start.1 = ((bf16[8,96,1024]{2,1,0:T(8,128)(2,1)}), bf16[8,96,1024]{2,1,0:T(8,128)(2,1)S(1)}, u32[]{:S(2)}, u32[]{:S(2)}) async-start(bf16[8,96,1024]{2,1,0:T(8,128)(2,1)} %select_select_fusion), calls=%async_computation.1 | async-start | bytes 3145728 | tf_op jit(solution)/shard_map/all_to_all | solution.py:46
  32.6 0.0 all-gather.2.cloned.1.call-start
  32.6 0.1 fusion.14
  32.7 0.2 reduce_window_sum.18
  32.8 0.2 select_reduce_fusion
  33.0 0.5 broadcast.229
  33.5 0.7 reduce.5
  34.2 0.1 eq.42
  34.3 17.3 %all-to-all-done.1 = bf16[8,96,1024]{2,1,0:T(8,128)(2,1)S(1)} async-done(((bf16[8,96,1024]{2,1,0:T(8,128)(2,1)}), bf16[8,96,1024]{2,1,0:T(8,128)(2,1)S(1)}, u32[]{:S(2)}, u32[]{:S(2)}) %all-to-all-start.1) | async-done | bytes 1572896 | tf_op jit(solution)/shard_map/all_to_all | solution.py:46
  51.6 0.0 copy-done.1
  51.6 0.5 multiply_reduce_fusion
  52.1 0.3 convolution_convert_fusion.1
  52.4 0.2 all_to_all.29
  52.7 43.2 %all_to_all.39 = bf16[64,3,1024]{2,1,0:T(4,128)(2,1)S(1)} all-to-all(bf16[64,3,1024]{2,1,0:T(4,128)(2,1)S(1)} %all_to_all.29), channel_id=1, replica_groups=mesh['dp'=8,'expert'=64] {'expert'}, dimensions={0} | all-to-all | bytes 786432 | tf_op jit(solution)/shard_map/all_to_all | solution.py:65
  95.9 1.1 all_to_all.31
  97.0 0.0 all-gather.2.cloned.1.call-update
  97.0 0.2 reduce-scatter.2.cloned.1.call-start
  97.2 0.0 copy-done.5
  97.3 0.0 copy-done.6
  97.3 29.6 %all-gather.2.cloned.1.call-done = bf16[1536,1024]{1,0:T(8,128)(2,1)} async-done(((bf16[192,1024]{1,0:T(8,128)(2,1)}), bf16[1536,1024]{1,0:T(8,128)(2,1)}) %all-gather.2.cloned.1.call-update) | async-done | bytes 3145744 | tf_op jit(solution)/shard_map/all_gather | solution.py:70
  127.0 0.6 broadcast_in_dim.67
  127.6 5.4 %fusion.5 = f32[1536,512]{1,0:T(8,128)} fusion(bf16[1536,1024]{1,0:T(8,128)(2,1)} %all-gather.2.cloned.1.call-done, bf16[64,8,8,128]{3,2,1,0:T(8,128)(2,1)S(1)} %bitcast.57, bf16[1,512,1024]{2,1,0:T(8,128)(2,1)S(1)} %copy-done.8), kind=kOutput, calls=%fused_computation.15 | convolution fusion | flops 1611137024 | bytes 8388608 | tf_op jit(solution)/shard_map/dot_general | solution.py:71
  133.1 0.6 broadcast_in_dim.69
  133.7 0.6 broadcast_in_dim.71
  134.3 8.9 %convolution_convert_fusion = bf16[1536,1024]{1,0:T(8,128)(2,1)} fusion(bf16[1536,1024]{1,0:T(8,128)(2,1)} %all-gather.2.cloned.1.call-done, f32[1536,512]{1,0:T(8,128)} %fusion.5, bf16[64,8,8,128]{3,2,1,0:T(8,128)(2,1)S(1)} %bitcast.56, bf16[64,8,8,128]{3,2,1,0:T(8,128)(2,1)S(1)} %bitcast.55, bf16[1,512,1024]{2,1,0:T(8,128)(2,1)} %param.20, ...), kind=kOutput, calls=%fused_computation.2 | convolution fusion | flops 3228565504 | bytes 13631488 | tf_op jit(solution)/shard_map/dot_general | solution.py:74
  143.2 0.0 reduce-scatter.2.cloned.1.call-update
  143.3 43.7 %reduce-scatter.2.cloned.1.call-done = bf16[192,1024]{1,0:T(8,128)(2,1)} async-done(((bf16[1536,1024]{1,0:T(8,128)(2,1)}), bf16[192,1024]{1,0:T(8,128)(2,1)}) %reduce-scatter.2.cloned.1.call-update) | async-done | bytes 393232 | tf_op jit(solution)/shard_map/reduce_scatter | solution.py:75
  187.0 1.4 all_to_all.32
  188.4 46.9 %all_to_all.40 = bf16[64,3,1024]{2,1,0:T(4,128)(2,1)S(1)} all-to-all(bf16[64,3,1024]{2,1,0:T(4,128)(2,1)S(1)} %all_to_all.32), channel_id=1, replica_groups=mesh['dp'=8,'expert'=64] {'expert'}, dimensions={0} | all-to-all | bytes 786432 | tf_op jit(solution)/shard_map/all_to_all | solution.py:78
  235.3 0.3 all_to_all.34
  235.6 1.0 fusion.1
  (20 shorter events, 0.1 us)
Async XLA Ops:
  6.5 16.8 %copy-start = (bf16[256,1024]{1,0:T(8,128)(2,1)S(1)}, bf16[256,1024]{1,0:T(8,128)(2,1)}, u32[]{:S(2)}) copy-start(bf16[256,1024]{1,0:T(8,128)(2,1)} %param.12) | copy-start | bytes 1572868
  6.5 6.6 %copy-start.7 = (s32[1,8]{1,0:T(1,128)S(1)}, s32[1,8]{1,0:T(1,128)}, u32[]{:S(2)}) copy-start(s32[1,8]{1,0:T(1,128)} %param.14) | copy-start | bytes 100
  13.9 13.8 %all-to-all-start = ((s32[8,96,1]{1,2,0:T(1,128)}), s32[8,96,1]{1,2,0:T(1,128)S(1)}, u32[]{:S(2)}, u32[]{:S(2)}) async-start(s32[8,96,1]{1,2,0:T(1,128)} %bitcast.3), calls=%async_computation | async-start | bytes 8192 | tf_op jit(solution)/shard_map/all_to_all | solution.py:47
  26.2 6.4 %copy-start.3 = (s32[128,1]{0,1:T(1,128)S(1)}, s32[128,1]{0,1:T(1,128)}, u32[]{:S(2)}) copy-start(s32[128,1]{0,1:T(1,128)} %param.17) | copy-start | bytes 1540
  26.2 25.4 %copy-start.1 = (bf16[128,1024]{1,0:T(8,128)(2,1)S(1)}, bf16[128,1024]{1,0:T(8,128)(2,1)}, u32[]{:S(2)}) copy-start(bf16[128,1024]{1,0:T(8,128)(2,1)} %param.15) | copy-start | bytes 786436
  27.6 24.4 %copy-start.2 = (f32[1024]{0:T(1024)S(1)}, f32[1024]{0:T(1024)}, u32[]{:S(2)}) copy-start(f32[1024]{0:T(1024)} %param.16) | copy-start | bytes 12292
  27.6 23.9 %all-to-all-start.1 = ((bf16[8,96,1024]{2,1,0:T(8,128)(2,1)}), bf16[8,96,1024]{2,1,0:T(8,128)(2,1)S(1)}, u32[]{:S(2)}, u32[]{:S(2)}) async-start(bf16[8,96,1024]{2,1,0:T(8,128)(2,1)} %select_select_fusion), calls=%async_computation.1 | async-start | bytes 3145728 | tf_op jit(solution)/shard_map/all_to_all | solution.py:46
  32.6 94.4 %all-gather.2.cloned.1.call-start = ((), (), s32[]{:S(2)}) async-start(), calls=%async_computation.5 | async-start | bytes 3538944 | tf_op jit(solution)/shard_map/all_gather | solution.py:70
  51.6 45.6 %copy-start.4 = (s32[1,4,8]{2,1,0:T(4,128)S(1)}, s32[1,4,8]{2,1,0:T(4,128)}, u32[]{:S(2)}) copy-start(s32[1,4,8]{2,1,0:T(4,128)} %param.21) | copy-start | bytes 388
  51.6 45.7 %copy-start.5 = (s32[1,4,8]{2,1,0:T(4,128)S(1)}, s32[1,4,8]{2,1,0:T(4,128)}, u32[]{:S(2)}) copy-start(s32[1,4,8]{2,1,0:T(4,128)} %param.22) | copy-start | bytes 388
  51.6 45.7 %copy-start.6 = (s32[1,4,8]{2,1,0:T(4,128)S(1)}, s32[1,4,8]{2,1,0:T(4,128)}, u32[]{:S(2)}) copy-start(s32[1,4,8]{2,1,0:T(4,128)} %param.23) | copy-start | bytes 388
  52.1 75.5 %copy-start.8 = (bf16[1,512,1024]{2,1,0:T(8,128)(2,1)S(1)}, bf16[1,512,1024]{2,1,0:T(8,128)(2,1)}, u32[]{:S(2)}) copy-start(bf16[1,512,1024]{2,1,0:T(8,128)(2,1)} %param.18) | copy-start | bytes 3145732
  97.0 90.0 %reduce-scatter.2.cloned.1.call-start = ((), (), s32[]{:S(2)}) async-start(), calls=%async_computation.6 | async-start | bytes 3538944 | tf_op jit(solution)/shard_map/reduce_scatter | solution.py:75
Sparse Core Ops, SparseCore 0:
  97.1 29.7 all-gather.1
  143.4 43.5 reduce-scatter.1
where the time goes:
time: 244 us; the launch traced here: 243 us
  waiting for transfers between devices  90.7 us (37%)
  blocking collectives  90.1 us (37%)
  matrix products  16.2 us (7%)
  starting transfers between devices  14.6 us (6%)
  between operations  13.6 us (6%)
  local copies, waits for them, and re-layouts  13.3 us (5%)
  other arithmetic  4.98 us (2%)
    all_to_all x1, blocking collectives, on_device(): lax.all_to_all(summed, 'expert', split_axis=0, concat_axis=0, tiled=True)  46.9 us
    reduce_scatter x1, waiting for transfers between devices, on_device(): lax.psum_scatter(partial_rows.astype(jnp.bfloat16), 'dp', scatter_dimensi...  43.7 us
    all_to_all x1, blocking collectives, on_device(): lax.all_to_all(outgoing, 'expert', split_axis=0, concat_axis=0, tiled=True)  43.2 us
    all_gather x1, waiting for transfers between devices, on_device(): block_rows = lax.all_gather(arrived, 'dp', axis=0, tiled=True)  29.6 us
    all_to_all x1, waiting for transfers between devices, on_device(): lax.all_to_all(slot_rows, 'dp', split_axis=0, concat_axis=0, tiled=True)  17.3 us
    all_to_all x1, starting transfers between devices, on_device(): lax.all_to_all(slot_bins, 'dp', split_axis=0, concat_axis=0, tiled=True)  9.41 us
    dot_general x1, matrix products, on_device(): partial_rows = jnp.dot(hidden, w_down, preferred_element_type=jnp.float32)  8.93 us
    dot_general x1, matrix products, on_device(): lax.dot_general(block_rows, w_gate, contract, preferred_element_type=jnp....  5.44 us
  transfers between devices with their start and end apart: 4, of which 3 were waited for; matrix products, arithmetic and copies ran while one was open for 2% of the time, Pallas kernels for 0%

commit v1 on v0

--- a/solution.py
+++ b/solution.py
@@ -67,7 +67,9 @@
     w_up = dequantize(up_q[0], up_scales[0])
     w_down = dequantize(down_q[0], down_scales[0])
     contract = (((1,), (1,)), ((), ()))
-    block_rows = lax.all_gather(arrived, "dp", axis=0, tiled=True)
+    block_rows = jnp.concatenate(
+        lax.all_to_all(jnp.stack([arrived] * lax.axis_size("dp")), "dp", 0, 0), axis=0
+    )
     gate_val = lax.dot_general(block_rows, w_gate, contract, preferred_element_type=jnp.float32)
     up_val = lax.dot_general(block_rows, w_up, contract, preferred_element_type=jnp.float32)
     hidden = (jax.nn.silu(gate_val) * up_val).astype(jnp.bfloat16)

time: 244 us -> 252 us (1.033)
  starting transfers between devices: 14.6 us -> 25 us
  waiting for transfers between devices: 90.7 us -> 84.4 us
  local copies, waits for them, and re-layouts: 13.3 us -> 16.5 us
    all_to_all x0 -> x1, waiting for transfers between devices: none -> 32.8 us  [on_device(): lax.all_to_all(jnp.stack([arrived] * lax.axis_size('dp')), 'dp', 0, 0)]
    all_gather x1 -> x0, waiting for transfers between devices: 29.6 us -> none  [on_device(): block_rows = lax.all_gather(arrived, 'dp', axis=0, tiled=True)]
    all_to_all x0 -> x1, starting transfers between devices: none -> 10.7 us  [on_device(): lax.all_to_all(jnp.stack([arrived] * lax.axis_size('dp')), 'dp', 0, 0)]
    reduce_scatter x1, waiting for transfers between devices: 43.7 us -> 34.3 us  [on_device(): lax.psum_scatter(partial_rows.astype(jnp.bfloat16), 'dp', scatter_dimensi...]
  transfers between devices with their start and end apart: 4 -> 4, of which waited for: 3 -> 3; matrix products, arithmetic and copies ran while one was open for 2% -> 4% of each run, Pallas kernels for 0% -> 0%
where the time goes in v1:
time: 252 us; the launch traced here: 251 us
  blocking collectives  90.2 us (36%)
  waiting for transfers between devices  84.4 us (33%)
  starting transfers between devices  25 us (10%)
  local copies, waits for them, and re-layouts  16.5 us (7%)
  matrix products  16.5 us (7%)
  between operations  13.6 us (5%)
  other arithmetic  4.98 us (2%)
    all_to_all x1, blocking collectives, on_device(): lax.all_to_all(summed, 'expert', split_axis=0, concat_axis=0, tiled=True)  46.9 us
    all_to_all x1, blocking collectives, on_device(): lax.all_to_all(outgoing, 'expert', split_axis=0, concat_axis=0, tiled=True)  43.2 us
    reduce_scatter x1, waiting for transfers between devices, on_device(): lax.psum_scatter(partial_rows.astype(jnp.bfloat16), 'dp', scatter_dimensi...  34.3 us
    all_to_all x1, waiting for transfers between devices, on_device(): lax.all_to_all(jnp.stack([arrived] * lax.axis_size('dp')), 'dp', 0, 0)  32.8 us
    all_to_all x1, waiting for transfers between devices, on_device(): lax.all_to_all(slot_rows, 'dp', split_axis=0, concat_axis=0, tiled=True)  17.3 us
    all_to_all x1, starting transfers between devices, on_device(): lax.all_to_all(jnp.stack([arrived] * lax.axis_size('dp')), 'dp', 0, 0)  10.7 us
    all_to_all x1, starting transfers between devices, on_device(): lax.all_to_all(slot_bins, 'dp', split_axis=0, concat_axis=0, tiled=True)  9.41 us
    dot_general x1, matrix products, on_device(): partial_rows = jnp.dot(hidden, w_down, preferred_element_type=jnp.float32)  8.91 us
  transfers between devices with their start and end apart: 4, of which 3 were waited for; matrix products, arithmetic and copies ran while one was open for 4% of the time, Pallas kernels for 0%

profile of v1, /device:TPU:7, one launch (start us, length us, event | category | flops | bytes accessed | tf_op | source)
XLA Modules:
  0.0 251.2 jit_solution(17387987381864511917)
XLA Ops:
  6.5 0.0 copy-start
  6.5 0.9 reduce-window.8
  7.4 0.7 bitcast_subtract_fusion
  8.1 0.1 add_clamp_fusion
  8.2 0.1 min.18
  8.3 4.8 %gather_fusion = s32[768]{0:T(1024)S(1)} fusion(s32[256]{0:T(256)} %param.13, s32[1024]{0:T(1024)S(1)} %pad_clamp_fusion), kind=kCustom, calls=%fused_computation | custom fusion | bytes 9216 | tf_op jit(solution)/shard_map/jit(_take)/gather | solution.py:44
  13.1 0.1 gather.13
  13.2 0.0 copy-done.8
  13.2 0.7 select_select_fusion.1
  13.9 9.4 %all-to-all-start = ((s32[8,96,1]{1,2,0:T(1,128)}), s32[8,96,1]{1,2,0:T(1,128)S(1)}, u32[]{:S(2)}, u32[]{:S(2)}) async-start(s32[8,96,1]{1,2,0:T(1,128)} %bitcast.3), calls=%async_computation | async-start | bytes 8192 | tf_op jit(solution)/shard_map/all_to_all | solution.py:47
  23.3 0.1 iota_compare_fusion.6
  23.3 0.0 copy-done
  23.3 2.8 %gather_fusion.1 = bf16[768,1024]{1,0:T(8,128)(2,1)S(1)} fusion(bf16[256,1024]{1,0:T(8,128)(2,1)S(1)} %copy-done, s32[1024]{0:T(1024)S(1)} %pad_clamp_fusion), kind=kCustom, calls=%fused_computation.1 | custom fusion | bytes 3148800 | tf_op jit(solution)/shard_map/jit(_take)/gather | solution.py:42
  26.2 0.0 copy-start.4
  26.2 0.0 copy-start.2
  26.2 1.5 select_select_fusion
  27.6 0.0 all-to-all-done
  27.6 4.9 %all-to-all-start.1 = ((bf16[8,96,1024]{2,1,0:T(8,128)(2,1)}), bf16[8,96,1024]{2,1,0:T(8,128)(2,1)S(1)}, u32[]{:S(2)}, u32[]{:S(2)}) async-start(bf16[8,96,1024]{2,1,0:T(8,128)(2,1)} %select_select_fusion), calls=%async_computation.1 | async-start | bytes 3145728 | tf_op jit(solution)/shard_map/all_to_all | solution.py:46
  32.6 0.1 fusion.14
  32.7 0.2 reduce_window_sum.18
  32.8 0.2 select_reduce_fusion
  33.0 0.5 broadcast.230
  33.5 0.7 reduce.5
  34.2 0.1 eq.42
  34.3 17.3 %all-to-all-done.1 = bf16[8,96,1024]{2,1,0:T(8,128)(2,1)S(1)} async-done(((bf16[8,96,1024]{2,1,0:T(8,128)(2,1)}), bf16[8,96,1024]{2,1,0:T(8,128)(2,1)S(1)}, u32[]{:S(2)}, u32[]{:S(2)}) %all-to-all-start.1) | async-done | bytes 1572896 | tf_op jit(solution)/shard_map/all_to_all | solution.py:46
  51.6 0.5 multiply_reduce_fusion
  52.1 0.3 convolution_convert_fusion.1
  52.4 0.2 all_to_all.30
  52.6 43.2 %all_to_all.41 = bf16[64,3,1024]{2,1,0:T(4,128)(2,1)S(1)} all-to-all(bf16[64,3,1024]{2,1,0:T(4,128)(2,1)S(1)} %all_to_all.30), channel_id=1, replica_groups=mesh['dp'=8,'expert'=64] {'expert'}, dimensions={0} | all-to-all | bytes 786432 | tf_op jit(solution)/shard_map/all_to_all | solution.py:65
  95.8 0.3 stack.4
  96.2 2.1 stack.5
  98.3 10.7 %all-to-all-start.3 = ((bf16[8,192,1024]{2,1,0:T(8,128)(2,1)}), bf16[8,192,1024]{2,1,0:T(8,128)(2,1)}, u32[]{:S(2)}, u32[]{:S(2)}) async-start(bf16[8,192,1024]{2,1,0:T(8,128)(2,1)} %stack.5), calls=%async_computation.3 | async-start | bytes 6291456 | tf_op jit(solution)/shard_map/all_to_all | solution.py:71
  109.0 0.0 reduce-scatter.2.cloned.1.call-start
  109.0 0.0 copy-start.7
  109.1 0.6 broadcast_in_dim.67
  109.7 0.5 convert_element_type.99
  110.2 0.6 broadcast_in_dim.69
  110.8 1.3 convert_element_type.104
  112.1 32.8 %all-to-all-done.3 = bf16[8,192,1024]{2,1,0:T(8,128)(2,1)} async-done(((bf16[8,192,1024]{2,1,0:T(8,128)(2,1)}), bf16[8,192,1024]{2,1,0:T(8,128)(2,1)}, u32[]{:S(2)}, u32[]{:S(2)}) %all-to-all-start.3) | async-done | bytes 3145760 | tf_op jit(solution)/shard_map/all_to_all | solution.py:71
  144.9 5.8 %fusion.6 = f32[1536,512]{1,0:T(8,128)} fusion(bf16[1536,1024]{1,0:T(8,128)(2,1)} %bitcast.7, bf16[1,512,1024]{2,1,0:T(8,128)(2,1)} %param.18, bf16[1,512,1024]{2,1,0:T(8,128)(2,1)S(1)} %convert_element_type.99), kind=kOutput, calls=%fused_computation.14 | convolution fusion | flops 1611137024 | bytes 8388608 | tf_op jit(solution)/shard_map/dot_general | solution.py:73
  150.8 0.6 broadcast_in_dim.71
  151.4 8.9 %convolution_convert_fusion = bf16[1536,1024]{1,0:T(8,128)(2,1)} fusion(bf16[1536,1024]{1,0:T(8,128)(2,1)} %bitcast.7, f32[1536,512]{1,0:T(8,128)} %fusion.6, bf16[64,8,8,128]{3,2,1,0:T(8,128)(2,1)S(1)} %bitcast.43, bf16[1,512,1024]{2,1,0:T(8,128)(2,1)} %param.20, bf16[1,512,1024]{2,1,0:T(8,128)(2,1)} %param.19, bf16[1,512,1024]{2,1,0:T(8,128)(2,1)S(1)} %copy-done.1), kind=kOutput, calls=%fused_computation.2 | convolution fusion | flops 3228565504 | bytes 13631488 | tf_op jit(solution)/shard_map/dot_general | solution.py:76
  160.3 0.0 reduce-scatter.2.cloned.1.call-update
  160.3 34.3 %reduce-scatter.2.cloned.1.call-done = bf16[192,1024]{1,0:T(8,128)(2,1)} async-done(((bf16[1536,1024]{1,0:T(8,128)(2,1)}), bf16[192,1024]{1,0:T(8,128)(2,1)}) %reduce-scatter.2.cloned.1.call-update) | async-done | bytes 393232 | tf_op jit(solution)/shard_map/reduce_scatter | solution.py:77
  194.6 1.4 all_to_all.33
  196.1 46.9 %all_to_all.42 = bf16[64,3,1024]{2,1,0:T(4,128)(2,1)S(1)} all-to-all(bf16[64,3,1024]{2,1,0:T(4,128)(2,1)S(1)} %all_to_all.33), channel_id=1, replica_groups=mesh['dp'=8,'expert'=64] {'expert'}, dimensions={0} | all-to-all | bytes 786432 | tf_op jit(solution)/shard_map/all_to_all | solution.py:80
  243.0 0.3 all_to_all.35
  243.3 1.0 fusion.1
  (22 shorter events, 0.1 us)
Async XLA Ops:
  6.5 16.8 %copy-start = (bf16[256,1024]{1,0:T(8,128)(2,1)S(1)}, bf16[256,1024]{1,0:T(8,128)(2,1)}, u32[]{:S(2)}) copy-start(bf16[256,1024]{1,0:T(8,128)(2,1)} %param.12) | copy-start | bytes 1572868
  6.5 6.6 %copy-start.8 = (s32[1,8]{1,0:T(1,128)S(1)}, s32[1,8]{1,0:T(1,128)}, u32[]{:S(2)}) copy-start(s32[1,8]{1,0:T(1,128)} %param.14) | copy-start | bytes 100
  13.9 13.8 %all-to-all-start = ((s32[8,96,1]{1,2,0:T(1,128)}), s32[8,96,1]{1,2,0:T(1,128)S(1)}, u32[]{:S(2)}, u32[]{:S(2)}) async-start(s32[8,96,1]{1,2,0:T(1,128)} %bitcast.3), calls=%async_computation | async-start | bytes 8192 | tf_op jit(solution)/shard_map/all_to_all | solution.py:47
  26.2 6.4 %copy-start.4 = (s32[128,1]{0,1:T(1,128)S(1)}, s32[128,1]{0,1:T(1,128)}, u32[]{:S(2)}) copy-start(s32[128,1]{0,1:T(1,128)} %param.17) | copy-start | bytes 1540
  26.2 25.4 %copy-start.2 = (bf16[128,1024]{1,0:T(8,128)(2,1)S(1)}, bf16[128,1024]{1,0:T(8,128)(2,1)}, u32[]{:S(2)}) copy-start(bf16[128,1024]{1,0:T(8,128)(2,1)} %param.15) | copy-start | bytes 786436
  27.6 24.4 %copy-start.3 = (f32[1024]{0:T(1024)S(1)}, f32[1024]{0:T(1024)}, u32[]{:S(2)}) copy-start(f32[1024]{0:T(1024)} %param.16) | copy-start | bytes 12292
  27.6 23.9 %all-to-all-start.1 = ((bf16[8,96,1024]{2,1,0:T(8,128)(2,1)}), bf16[8,96,1024]{2,1,0:T(8,128)(2,1)S(1)}, u32[]{:S(2)}, u32[]{:S(2)}) async-start(bf16[8,96,1024]{2,1,0:T(8,128)(2,1)} %select_select_fusion), calls=%async_computation.1 | async-start | bytes 3145728 | tf_op jit(solution)/shard_map/all_to_all | solution.py:46
  98.3 10.7 %copy-start.5 = (s32[1,4,8]{2,1,0:T(4,128)S(1)}, s32[1,4,8]{2,1,0:T(4,128)}, u32[]{:S(2)}) copy-start(s32[1,4,8]{2,1,0:T(4,128)} %param.21) | copy-start | bytes 388
  98.3 46.6 %all-to-all-start.3 = ((bf16[8,192,1024]{2,1,0:T(8,128)(2,1)}), bf16[8,192,1024]{2,1,0:T(8,128)(2,1)}, u32[]{:S(2)}, u32[]{:S(2)}) async-start(bf16[8,192,1024]{2,1,0:T(8,128)(2,1)} %stack.5), calls=%async_computation.3 | async-start | bytes 6291456 | tf_op jit(solution)/shard_map/all_to_all | solution.py:71
  109.0 1.2 copy-start.6
  109.0 85.6 %reduce-scatter.2.cloned.1.call-start = ((), (), s32[]{:S(2)}) async-start(), calls=%async_computation.6 | async-start | bytes 3538944 | tf_op jit(solution)/shard_map/reduce_scatter | solution.py:77
  109.0 3.1 %copy-start.7 = (s32[1,4,8]{2,1,0:T(4,128)S(1)}, s32[1,4,8]{2,1,0:T(4,128)}, u32[]{:S(2)}) copy-start(s32[1,4,8]{2,1,0:T(4,128)} %param.23) | copy-start | bytes 388
  144.9 6.4 %copy-start.1 = (bf16[1,512,1024]{2,1,0:T(8,128)(2,1)S(1)}, bf16[1,512,1024]{2,1,0:T(8,128)(2,1)}, u32[]{:S(2)}) copy-start(bf16[1,512,1024]{2,1,0:T(8,128)(2,1)} %convert_element_type.104) | copy-start | bytes 3145732
Sparse Core Ops, SparseCore 0:
  160.4 34.1 reduce-scatter.1
